TPU v7x, 512 devices: a whole 4x8x8 slice. The times are simulated.
512 devices in a mesh: seq: 32 (over y, x), head: 16 (over z, core).
Axes of the slice: x: 4, y: 8, z: 8, core: 2. Of those that a mesh axis runs over, the one named last changes fastest.
Arguments:
- inputs: bfloat16 [16384, 4096], P('seq', 'head'), may hold values from -6 to 6
- gate: bfloat16 [16384, 4096], P('seq', 'head'), may hold values from -6 to 6
- input_map: bfloat16 [128, 16384], P('head', 'seq'), may hold values from -3 to 3
- output_map: bfloat16 [128, 16384], P('head', 'seq'), may hold values from -3 to 3
- step: float32 [64, 16384], P('head', 'seq'), may hold values from 0.25 to 2
- decay_rate: float32 [64], P('head'), may hold values from 3e-05 to 0.03
- level_mix: float32 [9, 64, 16384], P(None, 'head', 'seq'), may hold values from 0.1 to 1
- skip: float32 [64], P('head'), may hold values from 0.25 to 0.75
- norm_gain: float32 [4096], P('head'), may hold values from 0.5 to 1.5
Outputs:
- normed: bfloat16 [16384, 4096], P('seq', 'head')
All inputs are finite; a program needn't handle non-finite values.
Results may differ from a plain program's by a relative error of at most 0.0075.
Values may be sent and summed in bfloat16 or wider, within the bound.
A program may use at most 64 MiB of HBM per device.

v0:
```python
import jax
import jax.numpy as jnp
import numpy as np
from jax import lax
from jax.sharding import PartitionSpec as P

HEADS = 64
P_SIZE = 64
N = 128
GROUP = 256
LEVELS = 9


def span_table(groups, group_bits):
    table = np.zeros((groups, max(group_bits, 1), groups), np.float32)
    for later in range(groups):
        if later >> 0 & 1:
            for earlier in range(groups):
                if earlier >> 0 == (later >> 0) - 1:
                    table[later, 0, earlier] = 1.0
    return table


def to_rows(array):
    return jnp.transpose(array, (1, 2, 0))[..., None]


def project_states(out_blocks, states):
    groups, levels, heads_here, width, size = states.shape
    flat = jnp.transpose(states, (0, 3, 1, 2, 4)).reshape(groups, width, levels * heads_here * size)
    high = flat.astype(jnp.bfloat16)
    low = (flat - high.astype(jnp.float32)).astype(jnp.bfloat16)
    paired = jnp.concatenate([high, low], axis=2)
    proj = jnp.einsum("nct,cnk->ctk", out_blocks, paired, preferred_element_type=jnp.float32)
    half = levels * heads_here * size
    proj = proj[:, :, :half] + proj[:, :, half:]
    return proj.reshape(groups, out_blocks.shape[2], levels, heads_here, size)


def on_device(inputs, gate, input_map, output_map, step, decay_rate, level_mix, skip, norm_gain):
    highest = lax.Precision.HIGHEST
    tokens = inputs.shape[0]
    heads_here = inputs.shape[1] // P_SIZE
    groups = tokens // GROUP
    group_bits = groups.bit_length() - 1
    in_map, out_map = (
        lax.all_gather(input_map, "head", axis=0, tiled=True),
        lax.all_gather(output_map, "head", axis=0, tiled=True),
    )
    log_decay = -step * decay_rate[:, None]
    step_blocks = step.reshape(heads_here, groups, GROUP)
    cum = jnp.cumsum(log_decay.reshape(heads_here, groups, GROUP), axis=2)
    in_blocks = in_map.reshape(N, groups, GROUP)
    out_blocks = out_map.reshape(N, groups, GROUP)
    values = inputs.reshape(groups, GROUP, heads_here, P_SIZE)
    scores = jnp.einsum("nct,ncs->cts", out_blocks, in_blocks, preferred_element_type=jnp.float32)
    rows = jnp.arange(GROUP, dtype=jnp.int32)
    causal = (rows[:, None] >= rows[None, :])[None, None]
    spread = cum[:, :, :, None] - cum[:, :, None, :]
    within = jnp.where(causal, jnp.exp(jnp.where(causal, spread, 0.0)), 0.0)
    weights = (scores[None] * within * step_blocks[:, :, None, :]).astype(jnp.bfloat16)
    intra = jnp.einsum("hcts,cshp->cthp", weights, values, preferred_element_type=jnp.float32)
    to_end = jnp.exp(cum[:, :, -1:] - cum) * step_blocks
    loads = (in_blocks[None] * to_end[:, None]).astype(jnp.bfloat16)
    group_states = jnp.einsum("hncs,cshp->chnp", loads, values, preferred_element_type=jnp.float32)
    totals = cum[:, :, -1]
    after = jnp.cumsum(totals, axis=1)
    before = after - totals
    mixed = level_mix.reshape(LEVELS, heads_here, groups, GROUP)
    local_spans = None
    member = jnp.asarray(span_table(groups, group_bits))[None] > 0.5
    gap = before[:, :, None, None] - after[:, None, None, :]
    mixing = jnp.where(member, jnp.exp(jnp.where(member, gap, 0.0)), 0.0)
    local_spans = jnp.einsum("hjbk,khnp->jbhnp", mixing, group_states, precision=highest)
    shard_state = jnp.einsum(
        "hk,khnp->hnp", jnp.exp(after[:, -1:] - after), group_states, precision=highest
    )
    shard_total = after[:, -1]
    rank = lax.axis_index("seq")
    seq_bits = lax.axis_size("seq").bit_length() - 1
    totals_all = lax.all_gather(shard_total[None], "seq", axis=0, tiled=True)
    ends = jnp.cumsum(totals_all, axis=0)
    starts = ends - totals_all
    mine = lax.dynamic_slice_in_dim(starts, rank, 1, 0)
    piece = lax.all_gather(shard_state[None], "seq", axis=0, tiled=True)
    count = piece.shape[0]
    index = jnp.arange(count, dtype=jnp.int32)
    flipped = jnp.bitwise_xor(index, rank)
    levels = jnp.stack([jnp.right_shift(flipped, level) == 1 for level in range(seq_bits)], axis=1)
    valid = (index < rank)[:, None]
    gap = mine - ends
    weight = jnp.where(valid, jnp.exp(jnp.where(valid, gap, 0.0)), 0.0)
    far_spans = jnp.einsum(
        "kb,kh,khnp->bhnp", levels.astype(jnp.float32), weight, piece, precision=highest
    )
    far_wide = jnp.broadcast_to(far_spans[None], (groups, seq_bits, heads_here, N, P_SIZE))
    all_states = jnp.concatenate([local_spans, far_wide], axis=1)
    proj = project_states(out_blocks, all_states)
    level = 0
    near = to_rows(mixed[1 + level]) * proj[:, :, level]
    far = jnp.zeros((groups, GROUP, heads_here, P_SIZE), jnp.float32)
    for level in range(seq_bits):
        far = far + to_rows(mixed[1 + group_bits + level]) * proj[:, :, group_bits + level]
    total = to_rows(mixed[0]) * intra
    total = total + to_rows(jnp.exp(cum)) * near
    total = total + to_rows(jnp.exp(cum + before[:, :, None])) * far
    total = total + skip[None, None, :, None] * values.astype(jnp.float32)
    gated = total.reshape(tokens, heads_here * P_SIZE) * jax.nn.silu(gate.astype(jnp.float32))
    squares = jnp.sum(gated * gated, axis=1)
    summed = lax.psum(squares, "head")
    scale = lax.rsqrt(summed / (HEADS * P_SIZE) + 1e-05)
    return (gated * scale[:, None] * norm_gain[None, :]).astype(jnp.bfloat16)


def solution(mesh):
    return jax.shard_map(
        on_device,
        mesh=mesh,
        in_specs=(
            P("seq", "head"),
            P("seq", "head"),
            P("head", "seq"),
            P("head", "seq"),
            P("head", "seq"),
            P("head"),
            P(None, "head", "seq"),
            P("head"),
            P("head"),
        ),
        out_specs=P("seq", "head"),
        check_vma=False,
    )
```

profile of v0, /device:TPU:1, one launch (start us, length us, event | category | flops | bytes accessed | tf_op | source)
XLA Modules:
  0.0 175.5 jit_solution(9207128223247510060)
XLA Ops:
  6.5 0.8 negate_multiply_fusion
  7.3 2.4 %reduce-window.6 = f32[4,2,2,128]{3,2,1,0:T(2,128)S(1)} reduce-window(f32[4,2,2,128]{3,2,1,0:T(2,128)S(1)} %reshape.198, f32[]{:T(128)} %constant.14.clone.1), window={size=1x1x1x128 pad=0_0x0_0x0_0x127_0}, to_apply=%region_0.0 | reduce-window | flops 260096 | bytes 16388 | tf_op jit(solution)/shard_map/reduce-window
  9.8 0.1 slice.85
  9.8 0.1 copy.157
  10.0 0.1 copy.158
  10.1 0.1 broadcast_add_fusion
  10.2 0.1 slice.87
  10.3 0.1 copy.204
  10.4 0.1 copy.168
  10.5 0.7 mul.157
  11.2 0.1 exponential_multiply_fusion
  11.4 1.2 reshape.216
  12.6 0.3 copy.163
  12.9 25.2 %all_gather.13 = bf16[128,512]{1,0:T(8,128)(2,1)S(1)} all-gather(bf16[8,512]{1,0:T(8,128)(2,1)} %param.12), channel_id=1, replica_groups=mesh['seq'=32,'head'=16] {'head'}, dimensions={0}, use_global_device_ids=true | all-gather | bytes 139264 | tf_op jit(solution)/shard_map/all_gather | solution.py:47
  38.1 0.1 copy.155
  38.2 0.1 copy.166
  38.3 1.0 multiply_reduce_fusion.1
  39.3 0.0 all-gather.4.cloned.1.call-update
  39.3 0.1 copy.172
  39.4 1.3 dynamic-slice
  41.3 0.1 fusion.51
  41.4 61.7 %all-reduce = f32[128]{0:T(128)S(1)} all-reduce(f32[128]{0:T(128)S(1)} %fusion.51), channel_id=2, replica_groups=mesh['seq'=32,'head'=16] {'seq'}, use_global_device_ids=true, to_apply=%add | all-reduce | flops 128 | bytes 1024
  103.1 0.1 reshape.204
  103.2 0.1 reduce_window_sum.54
  103.3 0.1 copy.171
  103.4 1.1 convolution_bitcast_fusion.2
  104.5 28.7 %all_gather.12 = bf16[128,512]{1,0:T(8,128)(2,1)S(1)} all-gather(bf16[8,512]{1,0:T(8,128)(2,1)S(1)} %copy-done.3), channel_id=1, replica_groups=mesh['seq'=32,'head'=16] {'head'}, dimensions={0}, use_global_device_ids=true | all-gather | bytes 139264 | tf_op jit(solution)/shard_map/all_gather | solution.py:48
  133.2 0.1 copy.154
  133.3 0.1 copy.192
  133.6 0.1 exponential_bitcast_fusion.1
  133.7 0.1 exponential_select_fusion
  133.8 0.2 fusion.53
  134.1 0.0 all-gather.4.cloned.1.call-done
  134.1 2.5 %broadcast_multiply_fusion = f32[32,4,128,64]{2,3,1,0:T(8,128)S(1)} fusion(f32[32,4,128,64]{2,3,1,0:T(8,128)} %bitcast.154, f32[32,4]{1,0:T(8,128)S(1)} %exponential_select_fusion), kind=kLoop, calls=%fused_computation.4 | loop fusion | flops 1048576 | bytes 8389120 | tf_op jit(solution)/shard_map/kb,kh,khnp->bhnp/dot_general | solution.py:93
  136.6 3.8 %fusion = f32[5,4,128,64]{2,0,3,1:T(8,128)S(1)} fusion(f32[32,4,128,64]{2,3,1,0:T(8,128)S(1)} %broadcast_multiply_fusion, pred[32,5]{0,1:T(8,128)(4,1)S(1)} %stack.2), kind=kOutput, calls=%fused_computation.1 | convolution fusion | flops 62914560 | bytes 4849824 | tf_op jit(solution)/shard_map/kb,kh,khnp->bhnp/dot_general | solution.py:93
  140.5 0.1 copy.175
  140.6 0.1 broadcast_in_dim.91
  140.7 0.2 pad_maximum_fusion
  140.9 0.2 fusion.5
  141.1 1.0 convolution_bitcast_fusion
  142.1 0.4 slice_add_fusion
  142.5 0.3 copy-done.2
  142.8 1.0 fusion.9
  143.9 0.4 copy.191
  144.3 0.2 multiply_reduce_fusion
  144.5 23.1 %psum.7 = f32[512]{0:T(512)S(1)} all-reduce(f32[512]{0:T(512)S(1)} %multiply_reduce_fusion), channel_id=1, replica_groups=mesh['seq'=32,'head'=16] {'head'}, use_global_device_ids=true, to_apply=%region_5.6 | all-reduce | flops 512 | bytes 4096 | tf_op jit(solution)/shard_map/psum | solution.py:110
  167.6 0.2 multiply_convert_fusion.4
  167.8 0.8 copy.193
  (35 shorter events, 0.4 us)
Async XLA Ops:
  6.5 96.8 %copy-start.6 = (pred[2,2]{1,0:T(4,128)(4,1)S(1)}, pred[2,2]{1,0:T(4,128)(4,1)}, u32[]{:S(2)}) copy-start(pred[2,2]{1,0:T(4,128)(4,1)} %constant.50) | copy-start | bytes 16
  6.5 127.5 %all-gather.4.cloned.1.call-start = ((), (), s32[]{:S(2)}) async-start(), calls=%async_computation | async-start | bytes 4325376 | tf_op jit(solution)/shard_map/all_gather | solution.py:85
  11.3 93.2 %copy-start.3 = (bf16[8,512]{1,0:T(8,128)(2,1)S(1)}, bf16[8,512]{1,0:T(8,128)(2,1)}, u32[]{:S(2)}) copy-start(bf16[8,512]{1,0:T(8,128)(2,1)} %param.13) | copy-start | bytes 24580
  12.6 120.7 %copy-start = (bf16[512,256]{1,0:T(8,128)(2,1)S(1)}, bf16[512,256]{1,0:T(8,128)(2,1)}, u32[]{:S(2)}) copy-start(bf16[512,256]{1,0:T(8,128)(2,1)} %param.11) | copy-start | bytes 786436
  12.9 120.9 %copy-start.1 = (f32[9,4,512]{2,1,0:T(4,128)S(1)}, f32[9,4,512]{2,1,0:T(4,128)}, u32[]{:S(2)}) copy-start(f32[9,4,512]{2,1,0:T(4,128)} %param.16) | copy-start | bytes 221188
  142.1 0.7 copy-start.2
  142.1 0.7 copy-start.5
  143.8 23.7 %copy-start.4 = (f32[256]{0:T(256)S(1)}, f32[256]{0:T(256)}, u32[]{:S(2)}) copy-start(f32[256]{0:T(256)} %param.18) | copy-start | bytes 3076
Sparse Core Ops, SparseCore 0:
  39.5 80.0 all-gather.3
where the time goes:
time: 176 us; the launch traced here: 175 us
  blocking collectives  139 us (79%)
  between operations  14.3 us (8%)
  matrix products  8.16 us (5%)
  other arithmetic  7.43 us (4%)
  local copies, waits for them, and re-layouts  6.88 us (4%)
    unnamed x1, blocking collectives  61.7 us
    all_gather x1, blocking collectives, on_device(): lax.all_gather(output_map, 'head', axis=0, tiled=True)  28.7 us
    all_gather x1, blocking collectives, on_device(): lax.all_gather(input_map, 'head', axis=0, tiled=True)  25.2 us
    psum x1, blocking collectives, on_device(): summed = lax.psum(squares, 'head')  23.1 us
    dot_general x1, matrix products, on_device(): jnp.einsum('kb,kh,khnp->bhnp', levels.astype(jnp.float32), weight, piece,...  3.83 us
  transfers between devices with their start and end apart: 1, of which 0 were waited for; matrix products, arithmetic and copies ran while one was open for 2% of the time, Pallas kernels for 0%

commit v1 on v0

--- a/solution.py
+++ b/solution.py
@@ -45,7 +45,9 @@
     group_bits = groups.bit_length() - 1
     in_map, out_map = (
         lax.all_gather(input_map, "head", axis=0, tiled=True),
-        lax.all_gather(output_map, "head", axis=0, tiled=True),
+        jnp.concatenate(
+            lax.all_to_all(jnp.stack([output_map] * lax.axis_size("head")), "head", 0, 0), axis=0
+        ),
     )
     log_decay = -step * decay_rate[:, None]
     step_blocks = step.reshape(heads_here, groups, GROUP)

time: 176 us -> 167 us (0.949)
  blocking collectives: 139 us -> 115 us
  waiting for transfers between devices: 0.04 us -> 10.1 us
  starting transfers between devices: 0.01 us -> 3.47 us
    all_gather x1 -> x0, blocking collectives: 28.7 us -> none  [on_device(): lax.all_gather(output_map, 'head', axis=0, tiled=True)]
    all_gather x1, waiting for transfers between devices: 0.02 us -> 10 us  [on_device(): piece = lax.all_gather(shard_state[None], 'seq', axis=0, tiled=True)]
    psum x1, blocking collectives: 23.1 us -> 28.1 us  [on_device(): summed = lax.psum(squares, 'head')]
    all_to_all x0 -> x1, starting transfers between devices: none -> 3.47 us  [on_device(): lax.all_to_all(jnp.stack([output_map] * lax.axis_size('head')), 'head', 0...]
  transfers between devices with their start and end apart: 1 -> 2, of which waited for: 0 -> 1; matrix products, arithmetic and copies ran while one was open for 2% -> 3% of each run, Pallas kernels for 0% -> 0%
where the time goes in v1:
time: 167 us; the launch traced here: 166 us
  blocking collectives  115 us (69%)
  between operations  14.3 us (9%)
  waiting for transfers between devices  10.1 us (6%)
  matrix products  8.14 us (5%)
  local copies, waits for them, and re-layouts  7.48 us (4%)
  other arithmetic  7.43 us (4%)
  starting transfers between devices  3.47 us (2%)
    unnamed x1, blocking collectives  61.9 us
    psum x1, blocking collectives, on_device(): summed = lax.psum(squares, 'head')  28.1 us
    all_gather x1, blocking collectives, on_device(): lax.all_gather(input_map, 'head', axis=0, tiled=True)  25.2 us
    all_gather x1, waiting for transfers between devices, on_device(): piece = lax.all_gather(shard_state[None], 'seq', axis=0, tiled=True)  10 us
    dot_general x1, matrix products, on_device(): jnp.einsum('kb,kh,khnp->bhnp', levels.astype(jnp.float32), weight, piece,...  3.83 us
    all_to_all x1, starting transfers between devices, on_device(): lax.all_to_all(jnp.stack([output_map] * lax.axis_size('head')), 'head', 0...  3.47 us
  transfers between devices with their start and end apart: 2, of which 1 were waited for; matrix products, arithmetic and copies ran while one was open for 3% of the time, Pallas kernels for 0%

profile of v1, /device:TPU:1, one launch (start us, length us, event | category | flops | bytes accessed | tf_op | source)
XLA Modules:
  0.0 166.1 jit_solution(8874883776886665836)
XLA Ops:
  6.5 0.8 negate_multiply_fusion
  7.3 2.4 %reduce-window.6 = f32[4,2,2,128]{3,2,1,0:T(2,128)S(1)} reduce-window(f32[4,2,2,128]{3,2,1,0:T(2,128)S(1)} %reshape.196, f32[]{:T(128)} %constant.14.clone.1), window={size=1x1x1x128 pad=0_0x0_0x0_0x127_0}, to_apply=%region_0.0 | reduce-window | flops 260096 | bytes 16388 | tf_op jit(solution)/shard_map/reduce-window
  9.8 0.1 slice.85
  9.9 0.1 copy.156
  10.0 0.1 copy.157
  10.1 0.1 broadcast_add_fusion
  10.2 0.1 slice.87
  10.3 0.1 copy.202
  10.4 0.1 copy.167
  10.5 0.7 mul.157
  11.3 0.1 exponential_multiply_fusion
  11.4 1.2 reshape.214
  12.6 0.3 copy.162
  12.9 25.2 %all_gather.9 = bf16[128,512]{1,0:T(8,128)(2,1)S(1)} all-gather(bf16[8,512]{1,0:T(8,128)(2,1)} %param.12), channel_id=1, replica_groups=mesh['seq'=32,'head'=16] {'head'}, dimensions={0}, use_global_device_ids=true | all-gather | bytes 139264 | tf_op jit(solution)/shard_map/all_gather | solution.py:47
  38.1 0.1 copy.153
  38.2 0.1 copy.165
  38.3 0.9 multiply_reduce_fusion.1
  39.3 0.0 all-gather.4.cloned.1.call-update
  39.3 0.7 stack.4
  40.0 3.5 %all-to-all-start = ((bf16[16,8,512]{2,1,0:T(8,128)(2,1)}), bf16[16,8,512]{2,1,0:T(8,128)(2,1)S(1)}, u32[]{:S(2)}, u32[]{:S(2)}) async-start(bf16[16,8,512]{2,1,0:T(8,128)(2,1)} %stack.4), calls=%async_computation | async-start | bytes 262144 | tf_op jit(solution)/shard_map/all_to_all | solution.py:49
  43.5 0.1 copy.171
  43.6 1.3 dynamic-slice
  45.5 0.1 fusion.54
  45.6 61.9 %all-reduce = f32[128]{0:T(128)S(1)} all-reduce(f32[128]{0:T(128)S(1)} %fusion.54), channel_id=2, replica_groups=mesh['seq'=32,'head'=16] {'seq'}, use_global_device_ids=true, to_apply=%add | all-reduce | flops 128 | bytes 1024
  107.4 0.1 reshape.202
  107.6 0.1 reduce_window_sum.54
  107.6 0.1 copy.170
  107.8 1.1 convolution_bitcast_fusion.2
  108.9 0.1 exponential_bitcast_fusion.1
  109.0 0.1 exponential_select_fusion
  109.1 0.1 copy.191
  109.4 0.3 fusion.36
  109.7 10.0 %all-gather.4.cloned.1.call-done = f32[128,128,64]{1,2,0:T(8,128)} async-done(((f32[4,128,64]{1,2,0:T(8,128)}), f32[128,128,64]{1,2,0:T(8,128)}) %all-gather.4.cloned.1.call-update) | async-done | bytes 4194320 | tf_op jit(solution)/shard_map/all_gather | solution.py:87
  119.7 2.5 %broadcast_multiply_fusion = f32[32,4,128,64]{2,3,1,0:T(8,128)S(1)} fusion(f32[32,4,128,64]{2,3,1,0:T(8,128)} %bitcast.151, f32[32,4]{1,0:T(8,128)S(1)} %exponential_select_fusion), kind=kLoop, calls=%fused_computation.4 | loop fusion | flops 1048576 | bytes 8389120 | tf_op jit(solution)/shard_map/kb,kh,khnp->bhnp/dot_general | solution.py:95
  122.2 3.8 %fusion = f32[5,4,128,64]{2,0,3,1:T(8,128)S(1)} fusion(f32[32,4,128,64]{2,3,1,0:T(8,128)S(1)} %broadcast_multiply_fusion, pred[32,5]{0,1:T(8,128)(4,1)S(1)} %stack.5), kind=kOutput, calls=%fused_computation.1 | convolution fusion | flops 62914560 | bytes 4849824 | tf_op jit(solution)/shard_map/kb,kh,khnp->bhnp/dot_general | solution.py:95
  126.1 0.1 copy.174
  126.2 0.1 broadcast_in_dim.91
  126.3 0.2 pad_maximum_fusion
  126.5 0.2 fusion.5
  126.7 1.0 convolution_bitcast_fusion
  127.7 0.4 slice_add_fusion
  128.1 0.3 copy-done.2
  128.4 1.0 fusion.9
  129.4 0.4 copy.190
  129.9 0.2 multiply_reduce_fusion
  130.1 28.1 %psum.7 = f32[512]{0:T(512)S(1)} all-reduce(f32[512]{0:T(512)S(1)} %multiply_reduce_fusion), channel_id=1, replica_groups=mesh['seq'=32,'head'=16] {'head'}, use_global_device_ids=true, to_apply=%region_5.6 | all-reduce | flops 512 | bytes 4096 | tf_op jit(solution)/shard_map/psum | solution.py:112
  158.2 0.2 multiply_convert_fusion.4
  158.4 0.8 copy.192
  (37 shorter events, 0.4 us)
Async XLA Ops:
  6.5 32.8 %copy-start.3 = (bf16[8,512]{1,0:T(8,128)(2,1)S(1)}, bf16[8,512]{1,0:T(8,128)(2,1)}, u32[]{:S(2)}) copy-start(bf16[8,512]{1,0:T(8,128)(2,1)} %param.13) | copy-start | bytes 24580
  6.5 113.2 %all-gather.4.cloned.1.call-start = ((), (), s32[]{:S(2)}) async-start(), calls=%async_computation.1 | async-start | bytes 4325376 | tf_op jit(solution)/shard_map/all_gather | solution.py:87
  7.3 100.5 %copy-start.6 = (pred[2,2]{1,0:T(4,128)(4,1)S(1)}, pred[2,2]{1,0:T(4,128)(4,1)}, u32[]{:S(2)}) copy-start(pred[2,2]{1,0:T(4,128)(4,1)} %constant.50) | copy-start | bytes 16
  12.6 96.5 %copy-start = (bf16[512,256]{1,0:T(8,128)(2,1)S(1)}, bf16[512,256]{1,0:T(8,128)(2,1)}, u32[]{:S(2)}) copy-start(bf16[512,256]{1,0:T(8,128)(2,1)} %param.11) | copy-start | bytes 786436
  12.9 96.4 %copy-start.1 = (f32[9,4,512]{2,1,0:T(4,128)S(1)}, f32[9,4,512]{2,1,0:T(4,128)}, u32[]{:S(2)}) copy-start(f32[9,4,512]{2,1,0:T(4,128)} %param.16) | copy-start | bytes 221188
  40.0 69.3 %all-to-all-start = ((bf16[16,8,512]{2,1,0:T(8,128)(2,1)}), bf16[16,8,512]{2,1,0:T(8,128)(2,1)S(1)}, u32[]{:S(2)}, u32[]{:S(2)}) async-start(bf16[16,8,512]{2,1,0:T(8,128)(2,1)} %stack.4), calls=%async_computation | async-start | bytes 262144 | tf_op jit(solution)/shard_map/all_to_all | solution.py:49
  127.7 0.7 copy-start.2
  127.7 0.7 copy-start.5
  129.4 28.8 %copy-start.4 = (f32[256]{0:T(256)S(1)}, f32[256]{0:T(256)}, u32[]{:S(2)}) copy-start(f32[256]{0:T(256)} %param.18) | copy-start | bytes 3076
Sparse Core Ops, SparseCore 0:
  39.4 80.2 all-gather.3
